TPU v7x, 256 devices: a whole 4x4x8 slice. The times are simulated.
256 devices in a mesh: mass: 32 (over x, z), sub: 8 (over y, core).
Axes of the slice: x: 4, y: 4, z: 8, core: 2. Of those that a mesh axis runs over, the one named last changes fastest.
Arguments:
- spectra: bfloat16 [32768, 4096], P(('mass', 'sub')), may hold values from -6 to 6
- w_in: bfloat16 [4096, 2048], P(None, 'sub'), may hold values from -0.09375 to 0.09375
- w_out: bfloat16 [2048, 512], P('sub'), may hold values from -0.125 to 0.125
- partner_rows: int32 [32, 8, 32, 8], P('mass', 'sub'), may hold values from 0 to 127
- pair_counts: int32 [32, 8, 32], P('mass', 'sub'), may hold values from 0 to 8, as said below
- pair_labels: int32 [32, 8, 32, 8], P('mass', 'sub'), may hold values from 0 to 1, as said below
Outputs:
- grad_in: float32 [4096, 2048], P('mass', 'sub')
- grad_out_t: float32 [512, 2048], P('mass', 'sub')
Inputs may be any that keep to these rules, and one draw needn't show every extreme that they name: pair_counts[m, s, q] equals pair_counts[q, s, m], is 0 for q = m, and at most 8; some count equals 8. pair_labels[m, s, q, c] equals pair_labels[q, s, m, c] for q != m.
All inputs are finite; a program needn't handle non-finite values.
Results may differ from a plain program's by a relative error of at most 0.0053.
Values may be sent and summed in bfloat16 or wider, within the bound.
A program may use at most 64 MiB of HBM per device.

v0:
```python
import jax
import jax.numpy as jnp
from jax import lax
from jax.sharding import PartitionSpec as P


def per_device(spectra, w_in, w_out, partner_rows, pair_counts, pair_labels):
    own_rows = spectra.shape[0]
    peers = partner_rows.shape[2]
    slots = partner_rows.shape[3]
    shard_rows = lax.all_gather(spectra, "sub", axis=0, tiled=True)
    pre = jnp.dot(shard_rows, w_in, preferred_element_type=jnp.float32)
    hidden = jax.nn.silu(pre).astype(jnp.bfloat16)
    embed = lax.psum_scatter(
        jnp.dot(hidden, w_out, preferred_element_type=jnp.float32),
        "sub",
        scatter_dimension=0,
        tiled=True,
    )
    norm = jnp.sqrt(jnp.sum(embed * embed, axis=-1, keepdims=True) + 1e-06)
    unit = embed / norm
    unit_b = unit.astype(jnp.bfloat16)
    flat_rows = partner_rows.reshape(peers * slots)
    selector = flat_rows[:, None] == jnp.arange(own_rows, dtype=jnp.int32)[None, :]
    mine = jnp.dot(
        selector.astype(jnp.bfloat16), unit_b, preferred_element_type=jnp.float32
    ).astype(jnp.bfloat16)
    outgoing = mine.reshape(peers, slots, mine.shape[1])
    incoming = lax.all_to_all(outgoing, "mass", split_axis=0, concat_axis=0, tiled=True)
    theirs = incoming.astype(jnp.float32)
    sim = jnp.sum(outgoing.astype(jnp.float32) * theirs, axis=-1)
    valid = jnp.arange(slots, dtype=jnp.int32)[None, :] < pair_counts.reshape(peers)[:, None]
    labels = pair_labels.reshape(peers, slots).astype(jnp.float32)
    coef = jnp.where(valid, 2.0 * (sim - labels), jnp.float32(0.0))
    weighted = (coef[..., None] * theirs).reshape(peers * slots, theirs.shape[2])
    grad_unit = lax.dot_general(
        selector.astype(jnp.float32),
        weighted,
        (((0,), (0,)), ((), ())),
        precision=lax.Precision.HIGHEST,
    )
    along = jnp.sum(unit * grad_unit, axis=-1, keepdims=True)
    grad_embed = ((grad_unit - unit * along) / norm).astype(jnp.bfloat16)
    grad_rows = lax.all_gather(grad_embed, "sub", axis=0, tiled=True)
    back = lax.dot_general(
        grad_rows, w_out, (((1,), (1,)), ((), ())), preferred_element_type=jnp.float32
    )
    gate = jax.nn.sigmoid(pre)
    grad_pre = (back * gate * (1.0 + pre * (1.0 - gate))).astype(jnp.bfloat16)
    out_part = lax.dot_general(
        grad_rows, hidden, (((0,), (0,)), ((), ())), preferred_element_type=jnp.float32
    )
    in_part = lax.dot_general(
        shard_rows, grad_pre, (((0,), (0,)), ((), ())), preferred_element_type=jnp.float32
    )
    n_mass = peers
    in_rows = in_part.shape[0] // n_mass
    out_rows = out_part.shape[0] // n_mass
    partial = jnp.concatenate(
        [
            in_part.reshape(n_mass, in_rows, in_part.shape[1]),
            out_part.reshape(n_mass, out_rows, out_part.shape[1]),
        ],
        axis=1,
    ).astype(jnp.bfloat16)
    summed = jnp.sum(
        lax.all_to_all(partial, "mass", split_axis=0, concat_axis=0, tiled=True).astype(
            jnp.float32
        ),
        axis=0,
    )
    grad_in, grad_out_t = (summed[:in_rows], summed[in_rows:])
    return (grad_in, grad_out_t)


def solution(mesh):
    placed = (
        P(("mass", "sub"), None),
        P(None, "sub"),
        P("sub", None),
        P("mass", "sub", None, None),
        P("mass", "sub", None),
        P("mass", "sub", None, None),
    )
    return jax.shard_map(
        per_device,
        mesh=mesh,
        in_specs=placed,
        out_specs=(P("mass", "sub"), P("mass", "sub")),
        check_vma=False,
    )
```

profile of v0, /device:TPU:32, one launch (start us, length us, event | category | flops | bytes accessed | tf_op | source)
XLA Modules:
  0.0 248.9 jit_solution(8469015729756273993)
XLA Ops:
  7.2 0.0 copy-start
  7.2 0.0 all-gather.3.cloned.1.call-start
  7.2 0.7 all-gather.3.cloned.1.call-update
  7.9 0.0 copy-start.7
  7.9 0.0 reduce-scatter.2.cloned.1.call-start
  8.0 56.8 %all-gather.3.cloned.1.call-done = bf16[1024,4096]{1,0:T(8,128)(2,1)} async-done(((bf16[128,4096]{1,0:T(8,128)(2,1)}), bf16[1024,4096]{1,0:T(8,128)(2,1)}) %all-gather.3.cloned.1.call-update) | async-done | bytes 8388624 | tf_op jit(solution)/shard_map/all_gather | solution.py:11
  64.8 0.0 copy-done
  64.8 5.7 %fusion.20 = f32[1024,256]{1,0:T(8,128)S(1)} fusion(bf16[1024,4096]{1,0:T(8,128)(2,1)} %all-gather.3.cloned.1.call-done, bf16[4096,256]{1,0:T(8,128)(2,1)S(1)} %copy-done), kind=kOutput, calls=%fused_computation.37 | convolution fusion | flops 2147483648 | bytes 11534336 | tf_op jit(solution)/shard_map/dot_general | solution.py:12
  70.5 0.0 copy-start.8
  70.5 1.0 copy-done.8
  71.5 0.0 copy-done.7
  71.5 0.0 copy-start.3
  71.5 1.8 fusion.19
  73.3 0.0 copy-start.4
  73.3 0.0 copy-start.5
  73.3 0.0 reduce-scatter.2.cloned.1.call-update
  73.4 0.0 copy-done.3
  73.4 0.1 copy.13
  73.4 0.1 eq.15
  73.5 36.3 %reduce-scatter.2.cloned.1.call-done = f32[128,512]{1,0:T(8,128)} async-done(((f32[1024,512]{1,0:T(8,128)}), f32[128,512]{1,0:T(8,128)}) %reduce-scatter.2.cloned.1.call-update) | async-done | bytes 262160 | tf_op jit(solution)/shard_map/reduce_scatter | solution.py:14
  109.9 0.0 copy-start.2
  109.9 1.1 multiply_reduce_fusion.1
  111.0 2.0 fusion.3
  113.0 10.1 %all-to-all-start = ((bf16[32,8,512]{2,1,0:T(8,128)(2,1)}), bf16[32,8,512]{2,1,0:T(8,128)(2,1)S(1)}, u32[]{:S(2)}, u32[]{:S(2)}) async-start(bf16[32,8,512]{2,1,0:T(8,128)(2,1)} %fusion.3), calls=%async_computation.1 | async-start | bytes 524288 | tf_op jit(solution)/shard_map/all_to_all | solution.py:29
  123.1 0.0 all-gather.5.cloned.1.call-start
  123.1 0.0 copy-done.4
  123.1 0.1 copy.14
  123.2 10.9 %all-to-all-done = bf16[32,8,512]{2,1,0:T(8,128)(2,1)S(1)} async-done(((bf16[32,8,512]{2,1,0:T(8,128)(2,1)}), bf16[32,8,512]{2,1,0:T(8,128)(2,1)S(1)}, u32[]{:S(2)}, u32[]{:S(2)}) %all-to-all-start) | async-done | bytes 262176 | tf_op jit(solution)/shard_map/all_to_all | solution.py:29
  134.1 1.1 fusion.7
  135.2 0.0 copy-done.5
  135.2 0.1 fusion.17
  135.3 1.5 multiply_reduce_fusion
  136.8 0.0 copy-done.2
  136.8 0.8 divide_convert_fusion
  137.6 0.0 all-gather.5.cloned.1.call-update
  137.6 20.8 %all-gather.5.cloned.1.call-done = bf16[1024,512]{1,0:T(8,128)(2,1)} async-done(((bf16[128,512]{1,0:T(8,128)(2,1)}), bf16[1024,512]{1,0:T(8,128)(2,1)}) %all-gather.5.cloned.1.call-update) | async-done | bytes 1048592 | tf_op jit(solution)/shard_map/all_gather | solution.py:44
  158.4 8.6 %fusion = bf16[4096,256]{0,1:T(8,128)(2,1)} fusion(bf16[1024,4096]{1,0:T(8,128)(2,1)} %all-gather.3.cloned.1.call-done, bf16[1024,512]{1,0:T(8,128)(2,1)} %all-gather.5.cloned.1.call-done, bf16[256,512]{1,0:T(8,128)(2,1)S(1)} %copy-done.7, f32[1024,256]{1,0:T(8,128)} %copy-done.8), kind=kOutput, calls=%fused_computation.1 | convolution fusion | flops 2419326976 | bytes 12845056 | tf_op jit(solution)/shard_map/dot_general | solution.py:53
  167.0 0.0 copy-start.6
  167.0 4.2 %copy.19 = bf16[4096,256]{1,0:T(8,128)(2,1)} copy(bf16[4096,256]{0,1:T(8,128)(2,1)} %fusion) | data formatting | bytes 4194304 | tf_op jit(solution)/shard_map/reshape | solution.py:61
  171.2 0.0 copy-done.6
  171.2 0.0 copy-start.1
  171.2 1.9 convolution_convert_fusion.1
  173.1 0.0 copy-done.1
  173.1 0.2 pad_maximum_fusion
  173.3 67.5 %all_to_all.10 = bf16[32,144,256]{2,1,0:T(8,128)(2,1)S(1)} all-to-all(bf16[32,144,256]{2,1,0:T(8,128)(2,1)S(1)} %pad_maximum_fusion), channel_id=1, replica_groups=mesh['mass'=32,'sub'=8] {'mass'}, dimensions={0} | all-to-all | bytes 4718592 | tf_op jit(solution)/shard_map/all_to_all | solution.py:67
  240.8 0.3 convert_reduce_fusion
  241.1 0.6 slice.9
  241.7 0.7 slice.8
  (1 shorter events, 0.0 us)
Async XLA Ops:
  7.2 57.6 %copy-start = (bf16[4096,256]{1,0:T(8,128)(2,1)S(1)}, bf16[4096,256]{1,0:T(8,128)(2,1)}, u32[]{:S(2)}) copy-start(bf16[4096,256]{1,0:T(8,128)(2,1)} %param.7) | copy-start | bytes 6291460
  7.2 57.6 %all-gather.3.cloned.1.call-start = ((), (), s32[]{:S(2)}) async-start(), calls=%async_computation.3 | async-start | bytes 9437184 | tf_op jit(solution)/shard_map/all_gather | solution.py:11
  7.9 63.6 %copy-start.7 = (bf16[256,512]{1,0:T(8,128)(2,1)S(1)}, bf16[256,512]{1,0:T(8,128)(2,1)}, u32[]{:S(2)}) copy-start(bf16[256,512]{1,0:T(8,128)(2,1)} %param.8) | copy-start | bytes 786436
  7.9 102.0 %reduce-scatter.2.cloned.1.call-start = ((), (), s32[]{:S(2)}) async-start(), calls=%async_computation.4 | async-start | bytes 2359296 | tf_op jit(solution)/shard_map/reduce_scatter | solution.py:14
  70.5 1.0 copy-start.8
  71.5 1.9 copy-start.3
  73.3 49.8 %copy-start.4 = (s32[1,1,32,8]{2,3,1,0:T(8,128)S(1)}, s32[1,1,32,8]{2,3,1,0:T(8,128)}, u32[]{:S(2)}) copy-start(s32[1,1,32,8]{2,3,1,0:T(8,128)} %param.11) | copy-start | bytes 3076
  73.3 61.9 %copy-start.5 = (s32[1,1,32]{2,1,0:T(1,128)S(1)}, s32[1,1,32]{2,1,0:T(1,128)}, u32[]{:S(2)}) copy-start(s32[1,1,32]{2,1,0:T(1,128)} %param.10) | copy-start | bytes 388
  109.9 26.9 %copy-start.2 = (f32[128,512]{1,0:T(8,128)S(1)}, f32[128,512]{1,0:T(8,128)}, u32[]{:S(2)}) copy-start(f32[128,512]{1,0:T(8,128)} %reduce-scatter.2.cloned.1.call-done) | copy-start | bytes 786436
  113.0 21.1 %all-to-all-start = ((bf16[32,8,512]{2,1,0:T(8,128)(2,1)}), bf16[32,8,512]{2,1,0:T(8,128)(2,1)S(1)}, u32[]{:S(2)}, u32[]{:S(2)}) async-start(bf16[32,8,512]{2,1,0:T(8,128)(2,1)} %fusion.3), calls=%async_computation.1 | async-start | bytes 524288 | tf_op jit(solution)/shard_map/all_to_all | solution.py:29
  123.1 35.3 %all-gather.5.cloned.1.call-start = ((), (), s32[]{:S(2)}) async-start(), calls=%async_computation.5 | async-start | bytes 1179648 | tf_op jit(solution)/shard_map/all_gather | solution.py:44
  167.0 4.2 %copy-start.6 = (bf16[1024,512]{1,0:T(8,128)(2,1)S(1)}, bf16[1024,512]{1,0:T(8,128)(2,1)}, u32[]{:S(2)}) copy-start(bf16[1024,512]{1,0:T(8,128)(2,1)} %all-gather.5.cloned.1.call-done) | copy-start | bytes 3145732
  171.2 2.0 copy-start.1
Sparse Core Ops, SparseCore 0:
  9.9 54.8 all-gather.2
  73.5 36.3 reduce-scatter.1
  137.7 20.6 all-gather.4
where the time goes:
time: 249 us
  waiting for transfers between devices  126 us (51%)
  blocking collectives  67.5 us (27%)
  matrix products  21.5 us (9%)
  between operations  13.9 us (6%)
  starting transfers between devices  10.2 us (4%)
  local copies, waits for them, and re-layouts  6.69 us (3%)
  other arithmetic  3.58 us (1%)
    all_to_all x1, blocking collectives, per_device(): lax.all_to_all(partial, 'mass', split_axis=0, concat_axis=0, tiled=True)  67.5 us
    all_gather x1, waiting for transfers between devices, per_device(): shard_rows = lax.all_gather(spectra, 'sub', axis=0, tiled=True)  56.8 us
    reduce_scatter x1, waiting for transfers between devices, per_device(): lax.psum_scatter(jnp.dot(hidden, w_out, preferred_element_type=jnp.float3...  36.3 us
    all_gather x1, waiting for transfers between devices, per_device(): grad_rows = lax.all_gather(grad_embed, 'sub', axis=0, tiled=True)  20.8 us
    all_to_all x1, waiting for transfers between devices, per_device(): lax.all_to_all(outgoing, 'mass', split_axis=0, concat_axis=0, tiled=True)  10.9 us
    all_to_all x1, starting transfers between devices, per_device(): lax.all_to_all(outgoing, 'mass', split_axis=0, concat_axis=0, tiled=True)  10.1 us
    dot_general x1, matrix products, per_device(): lax.dot_general(shard_rows, grad_pre, (((0,), (0,)), ((), ())), preferred...  8.59 us
    dot_general x1, matrix products, per_device(): pre = jnp.dot(shard_rows, w_in, preferred_element_type=jnp.float32)  5.71 us
  transfers between devices with their start and end apart: 4, of which 4 were waited for; matrix products, arithmetic and copies ran while one was open for 0% of the time, Pallas kernels for 0%

commit v1 on v0

--- a/solution.py
+++ b/solution.py
@@ -41,7 +41,31 @@
     )
     along = jnp.sum(unit * grad_unit, axis=-1, keepdims=True)
     grad_embed = ((grad_unit - unit * along) / norm).astype(jnp.bfloat16)
-    grad_rows = lax.all_gather(grad_embed, "sub", axis=0, tiled=True)
+    inter, r2, z1 = (lax.axis_size("sub"), lax.axis_index("sub"), grad_embed.shape[0])
+    grad_rows = lax.dynamic_update_slice_in_dim(
+        jnp.zeros(
+            tuple((tick * inter if u == 0 else tick for u, tick in enumerate(grad_embed.shape))),
+            grad_embed.dtype,
+        ),
+        grad_embed,
+        r2 * z1,
+        axis=0,
+    )
+    res = answer = grad_embed
+    dev_i = 1
+    while dev_i < inter // 2 + 1:
+        res = lax.ppermute(res, "sub", tuple(((u, (u + 1) % inter) for u in range(inter))))
+        grad_rows = lax.dynamic_update_slice_in_dim(
+            grad_rows, res, (r2 - dev_i) % inter * z1, axis=0
+        )
+        if 2 * dev_i < inter:
+            answer = lax.ppermute(
+                answer, axis_name="sub", perm=tuple(((u, (u - 1) % inter) for u in range(inter)))
+            )
+            grad_rows = lax.dynamic_update_slice_in_dim(
+                grad_rows, answer, (r2 + dev_i) % inter * z1, axis=0
+            )
+        dev_i = dev_i + 1
     back = lax.dot_general(
         grad_rows, w_out, (((1,), (1,)), ((), ())), preferred_element_type=jnp.float32
     )

time: 249 us -> 241 us (0.968)
  blocking collectives: 67.5 us -> 57.3 us
  starting transfers between devices: 10.2 us -> 19 us
  waiting for transfers between devices: 126 us -> 118 us
    all_gather x1 -> x0, waiting for transfers between devices: 20.8 us -> none  [per_device(): grad_rows = lax.all_gather(grad_embed, 'sub', axis=0, tiled=True)]
    ppermute x0 -> x7, waiting for transfers between devices: none -> 13.4 us  [the longest x4 13.4 us: per_device(): lax.ppermute(res, 'sub', tuple(((u, (u + 1) % inter) for u in range(inter...]
    all_to_all x1, blocking collectives: 67.5 us -> 57.3 us  [per_device(): lax.all_to_all(partial, 'mass', split_axis=0, concat_axis=0, tiled=True)]
    ppermute x0 -> x7, starting transfers between devices: none -> 8.88 us  [the longest x3 8.85 us: per_device(): lax.ppermute(answer, axis_name='sub', perm=tuple(((u, (u - 1) % inter) fo...]
  transfers between devices with their start and end apart: 4 -> 10, of which waited for: 4 -> 7; matrix products, arithmetic and copies ran while one was open for 0% -> 0% of each run, Pallas kernels for 0% -> 0%
where the time goes in v1:
time: 241 us; the launch traced here: 240 us
  waiting for transfers between devices  118 us (49%)
  blocking collectives  57.3 us (24%)
  matrix products  21.2 us (9%)
  starting transfers between devices  19 us (8%)
  between operations  14.2 us (6%)
  local copies, waits for them, and re-layouts  5.79 us (2%)
  other arithmetic  4.51 us (2%)
    all_to_all x1, blocking collectives, per_device(): lax.all_to_all(partial, 'mass', split_axis=0, concat_axis=0, tiled=True)  57.3 us
    all_gather x1, waiting for transfers between devices, per_device(): shard_rows = lax.all_gather(spectra, 'sub', axis=0, tiled=True)  56.8 us
    reduce_scatter x1, waiting for transfers between devices, per_device(): lax.psum_scatter(jnp.dot(hidden, w_out, preferred_element_type=jnp.float3...  36.3 us
    ppermute x4, waiting for transfers between devices, per_device(): lax.ppermute(res, 'sub', tuple(((u, (u + 1) % inter) for u in range(inter...  13.4 us
    all_to_all x1, waiting for transfers between devices, per_device(): lax.all_to_all(outgoing, 'mass', split_axis=0, concat_axis=0, tiled=True)  11 us
    all_to_all x1, starting transfers between devices, per_device(): lax.all_to_all(outgoing, 'mass', split_axis=0, concat_axis=0, tiled=True)  10 us
    ppermute x3, starting transfers between devices, per_device(): lax.ppermute(answer, axis_name='sub', perm=tuple(((u, (u - 1) % inter) fo...  8.85 us
    dot_general x1, matrix products, per_device(): lax.dot_general(shard_rows, grad_pre, (((0,), (0,)), ((), ())), preferred...  8.36 us
  transfers between devices with their start and end apart: 10, of which 7 were waited for; matrix products, arithmetic and copies ran while one was open for 0% of the time, Pallas kernels for 0%

profile of v1, /device:TPU:32, one launch (start us, length us, event | category | flops | bytes accessed | tf_op | source)
XLA Modules:
  0.0 240.3 jit_solution(198959262908838978)
XLA Ops:
  7.2 0.0 copy-start
  7.2 0.0 all-gather.2.cloned.1.call-start
  7.2 0.7 all-gather.2.cloned.1.call-update
  7.9 0.0 copy-start.5
  7.9 0.0 reduce-scatter.2.cloned.1.call-start
  8.0 56.8 %all-gather.2.cloned.1.call-done = bf16[1024,4096]{1,0:T(8,128)(2,1)} async-done(((bf16[128,4096]{1,0:T(8,128)(2,1)}), bf16[1024,4096]{1,0:T(8,128)(2,1)}) %all-gather.2.cloned.1.call-update) | async-done | bytes 8388624 | tf_op jit(solution)/shard_map/all_gather | solution.py:11
  64.8 0.0 copy-done
  64.8 5.7 %fusion.20 = f32[1024,256]{1,0:T(8,128)S(1)} fusion(bf16[1024,4096]{1,0:T(8,128)(2,1)} %all-gather.2.cloned.1.call-done, bf16[4096,256]{1,0:T(8,128)(2,1)S(1)} %copy-done), kind=kOutput, calls=%fused_computation.45 | convolution fusion | flops 2147483648 | bytes 11534336 | tf_op jit(solution)/shard_map/dot_general | solution.py:12
  70.5 0.0 copy-done.5
  70.5 0.0 copy-start.6
  70.6 0.0 copy-start.2
  70.6 1.8 fusion.19
  72.4 0.0 copy-done.6
  72.4 0.0 copy-start.3
  72.4 0.0 copy-start.4
  72.4 0.0 reduce-scatter.2.cloned.1.call-update
  72.4 0.0 copy-done.2
  72.4 0.1 copy.13
  72.5 0.1 eq.23
  72.6 36.3 %reduce-scatter.2.cloned.1.call-done = f32[128,512]{1,0:T(8,128)} async-done(((f32[1024,512]{1,0:T(8,128)}), f32[128,512]{1,0:T(8,128)}) %reduce-scatter.2.cloned.1.call-update) | async-done | bytes 262160 | tf_op jit(solution)/shard_map/reduce_scatter | solution.py:14
  108.9 0.0 copy-start.1
  108.9 1.1 multiply_reduce_fusion.1
  110.1 2.0 fusion.3
  112.1 10.0 %all-to-all-start = ((bf16[32,8,512]{2,1,0:T(8,128)(2,1)}), bf16[32,8,512]{2,1,0:T(8,128)(2,1)S(1)}, u32[]{:S(2)}, u32[]{:S(2)}) async-start(bf16[32,8,512]{2,1,0:T(8,128)(2,1)} %fusion.3), calls=%async_computation.1 | async-start | bytes 524288 | tf_op jit(solution)/shard_map/all_to_all | solution.py:29
  122.1 0.0 copy-done.3
  122.1 0.1 copy.14
  122.2 11.0 %all-to-all-done = bf16[32,8,512]{2,1,0:T(8,128)(2,1)S(1)} async-done(((bf16[32,8,512]{2,1,0:T(8,128)(2,1)}), bf16[32,8,512]{2,1,0:T(8,128)(2,1)S(1)}, u32[]{:S(2)}, u32[]{:S(2)}) %all-to-all-start) | async-done | bytes 262176 | tf_op jit(solution)/shard_map/all_to_all | solution.py:29
  133.2 1.1 fusion.7
  134.3 0.0 copy-done.4
  134.3 0.1 fusion.17
  134.3 1.5 multiply_reduce_fusion
  135.8 0.1 broadcast_in_dim.6
  135.9 0.0 copy-done.1
  135.9 0.1 constant_dynamic-update-slice_fusion.7
  136.0 0.0 collective-permute-start
  136.1 2.9 %collective-permute-start.1 = (bf16[128,512]{1,0:T(8,128)(2,1)S(1)}, bf16[128,512]{1,0:T(8,128)(2,1)S(1)}, u32[]{:S(2)}, u32[]{:S(2)}) collective-permute-start(bf16[128,512]{1,0:T(8,128)(2,1)S(1)} %get-tuple-element.5), channel_id=1, source_target_pairs={{0,7},{1,0},{2,1},{3,2},{4,3},{5,4},{6,5},{7,6},{8,15},{9,8},{10,9... | collective-permute-start | bytes 393224 | tf_op jit(solution)/shard_map/ppermute | solution.py:62
  139.0 2.6 %collective-permute-done = bf16[128,512]{1,0:T(8,128)(2,1)S(1)} collective-permute-done((bf16[128,512]{1,0:T(8,128)(2,1)S(1)}, bf16[128,512]{1,0:T(8,128)(2,1)S(1)}, u32[]{:S(2)}, u32[]{:S(2)}) %collective-permute-start) | collective-permute-done | bytes 131104 | tf_op jit(solution)/shard_map/ppermute | solution.py:57
  141.7 0.0 collective-permute-start.2
  141.7 0.0 collective-permute-done.1
  141.7 3.0 %collective-permute-start.3 = (bf16[128,512]{1,0:T(8,128)(2,1)S(1)}, bf16[128,512]{1,0:T(8,128)(2,1)S(1)}, u32[]{:S(2)}, u32[]{:S(2)}) collective-permute-start(bf16[128,512]{1,0:T(8,128)(2,1)S(1)} %collective-permute-done.1), channel_id=1, source_target_pairs={{0,7},{1,0},{2,1},{3,2},{4,3},{5,4},{6,5},{7,6},{8,15},{9,8},{10,9... | collective-permute-start | bytes 393224 | tf_op jit(solution)/shard_map/ppermute | solution.py:62
  144.7 2.6 %collective-permute-done.2 = bf16[128,512]{1,0:T(8,128)(2,1)S(1)} collective-permute-done((bf16[128,512]{1,0:T(8,128)(2,1)S(1)}, bf16[128,512]{1,0:T(8,128)(2,1)S(1)}, u32[]{:S(2)}, u32[]{:S(2)}) %collective-permute-start.2) | collective-permute-done | bytes 131104 | tf_op jit(solution)/shard_map/ppermute | solution.py:57
  147.3 0.0 collective-permute-start.4
  147.3 0.0 collective-permute-done.3
  147.3 3.0 %collective-permute-start.5 = (bf16[128,512]{1,0:T(8,128)(2,1)S(1)}, bf16[128,512]{1,0:T(8,128)(2,1)S(1)}, u32[]{:S(2)}, u32[]{:S(2)}) collective-permute-start(bf16[128,512]{1,0:T(8,128)(2,1)S(1)} %collective-permute-done.3), channel_id=1, source_target_pairs={{0,7},{1,0},{2,1},{3,2},{4,3},{5,4},{6,5},{7,6},{8,15},{9,8},{10,9... | collective-permute-start | bytes 393224 | tf_op jit(solution)/shard_map/ppermute | solution.py:62
  150.3 2.6 %collective-permute-done.4 = bf16[128,512]{1,0:T(8,128)(2,1)S(1)} collective-permute-done((bf16[128,512]{1,0:T(8,128)(2,1)S(1)}, bf16[128,512]{1,0:T(8,128)(2,1)S(1)}, u32[]{:S(2)}, u32[]{:S(2)}) %collective-permute-start.4) | collective-permute-done | bytes 131104 | tf_op jit(solution)/shard_map/ppermute | solution.py:57
  152.9 0.0 collective-permute-start.6
  152.9 0.0 collective-permute-done.5
  152.9 5.5 %collective-permute-done.6 = bf16[128,512]{1,0:T(8,128)(2,1)S(1)} collective-permute-done((bf16[128,512]{1,0:T(8,128)(2,1)S(1)}, bf16[128,512]{1,0:T(8,128)(2,1)S(1)}, u32[]{:S(2)}, u32[]{:S(2)}) %collective-permute-start.6) | collective-permute-done | bytes 131104 | tf_op jit(solution)/shard_map/ppermute | solution.py:57
  158.5 1.8 convolution_convert_fusion.1
  160.3 8.4 %fusion = bf16[4096,256]{0,1:T(8,128)(2,1)} fusion(bf16[1024,4096]{1,0:T(8,128)(2,1)} %all-gather.2.cloned.1.call-done, bf16[1024,512]{1,0:T(8,128)(2,1)S(1)} %constant_dynamic-update-slice_fusion, bf16[256,512]{1,0:T(8,128)(2,1)} %param.8, f32[1024,256]{1,0:T(8,128)} %copy-done.6), kind=kOutput, calls=%fused_computation.1 | convolution fusion | flops 2419326976 | bytes 12845056 | tf_op jit(solution)/shard_map/dot_general | solution.py:77
  168.6 4.1 %copy.19 = bf16[4096,256]{1,0:T(8,128)(2,1)} copy(bf16[4096,256]{0,1:T(8,128)(2,1)} %fusion) | data formatting | bytes 4194304 | tf_op jit(solution)/shard_map/reshape | solution.py:85
  172.7 1.8 pad_maximum_fusion
  174.5 57.3 %all_to_all.10 = bf16[32,144,256]{2,1,0:T(8,128)(2,1)S(1)} all-to-all(bf16[32,144,256]{2,1,0:T(8,128)(2,1)S(1)} %pad_maximum_fusion), channel_id=1, replica_groups=mesh['mass'=32,'sub'=8] {'mass'}, dimensions={0} | all-to-all | bytes 4718592 | tf_op jit(solution)/shard_map/all_to_all | solution.py:91
  231.8 0.3 convert_reduce_fusion
  232.2 0.7 slice.8
  232.8 0.6 slice.9
  (8 shorter events, 0.1 us)
Async XLA Ops:
  7.2 57.6 %copy-start = (bf16[4096,256]{1,0:T(8,128)(2,1)S(1)}, bf16[4096,256]{1,0:T(8,128)(2,1)}, u32[]{:S(2)}) copy-start(bf16[4096,256]{1,0:T(8,128)(2,1)} %param.7) | copy-start | bytes 6291460
  7.2 57.6 %all-gather.2.cloned.1.call-start = ((), (), s32[]{:S(2)}) async-start(), calls=%async_computation.3 | async-start | bytes 9437184 | tf_op jit(solution)/shard_map/all_gather | solution.py:11
  7.9 62.6 %copy-start.5 = (bf16[256,512]{1,0:T(8,128)(2,1)S(1)}, bf16[256,512]{1,0:T(8,128)(2,1)}, u32[]{:S(2)}) copy-start(bf16[256,512]{1,0:T(8,128)(2,1)} %param.8) | copy-start | bytes 786436
  7.9 101.0 %reduce-scatter.2.cloned.1.call-start = ((), (), s32[]{:S(2)}) async-start(), calls=%async_computation.4 | async-start | bytes 2359296 | tf_op jit(solution)/shard_map/reduce_scatter | solution.py:14
  70.5 1.9 copy-start.6
  70.6 1.9 copy-start.2
  72.4 49.7 %copy-start.3 = (s32[1,1,32,8]{2,3,1,0:T(8,128)S(1)}, s32[1,1,32,8]{2,3,1,0:T(8,128)}, u32[]{:S(2)}) copy-start(s32[1,1,32,8]{2,3,1,0:T(8,128)} %param.11) | copy-start | bytes 3076
  72.4 61.9 %copy-start.4 = (s32[1,1,32]{2,1,0:T(1,128)S(1)}, s32[1,1,32]{2,1,0:T(1,128)}, u32[]{:S(2)}) copy-start(s32[1,1,32]{2,1,0:T(1,128)} %param.10) | copy-start | bytes 388
  108.9 27.0 %copy-start.1 = (f32[128,512]{1,0:T(8,128)S(1)}, f32[128,512]{1,0:T(8,128)}, u32[]{:S(2)}) copy-start(f32[128,512]{1,0:T(8,128)} %reduce-scatter.2.cloned.1.call-done) | copy-start | bytes 786436
  112.1 21.1 %all-to-all-start = ((bf16[32,8,512]{2,1,0:T(8,128)(2,1)}), bf16[32,8,512]{2,1,0:T(8,128)(2,1)S(1)}, u32[]{:S(2)}, u32[]{:S(2)}) async-start(bf16[32,8,512]{2,1,0:T(8,128)(2,1)} %fusion.3), calls=%async_computation.1 | async-start | bytes 524288 | tf_op jit(solution)/shard_map/all_to_all | solution.py:29
  136.0 5.6 %collective-permute-start = (bf16[128,512]{1,0:T(8,128)(2,1)S(1)}, bf16[128,512]{1,0:T(8,128)(2,1)S(1)}, u32[]{:S(2)}, u32[]{:S(2)}) collective-permute-start(bf16[128,512]{1,0:T(8,128)(2,1)S(1)} %get-tuple-element.5), channel_id=1, source_target_pairs={{0,1},{1,2},{2,3},{3,4},{4,5},{5,6},{6,7},{7,0},{8,9},{9,10},{10,1... | collective-permute-start | bytes 393224 | tf_op jit(solution)/shard_map/ppermute | solution.py:57
  136.1 5.6 %collective-permute-start.1 = (bf16[128,512]{1,0:T(8,128)(2,1)S(1)}, bf16[128,512]{1,0:T(8,128)(2,1)S(1)}, u32[]{:S(2)}, u32[]{:S(2)}) collective-permute-start(bf16[128,512]{1,0:T(8,128)(2,1)S(1)} %get-tuple-element.5), channel_id=1, source_target_pairs={{0,7},{1,0},{2,1},{3,2},{4,3},{5,4},{6,5},{7,6},{8,15},{9,8},{10,9... | collective-permute-start | bytes 393224 | tf_op jit(solution)/shard_map/ppermute | solution.py:62
  141.7 5.6 %collective-permute-start.2 = (bf16[128,512]{1,0:T(8,128)(2,1)S(1)}, bf16[128,512]{1,0:T(8,128)(2,1)S(1)}, u32[]{:S(2)}, u32[]{:S(2)}) collective-permute-start(bf16[128,512]{1,0:T(8,128)(2,1)S(1)} %collective-permute-done), channel_id=1, source_target_pairs={{0,1},{1,2},{2,3},{3,4},{4,5},{5,6},{6,7},{7,0},{8,9},{9,10},{10,1... | collective-permute-start | bytes 393224 | tf_op jit(solution)/shard_map/ppermute | solution.py:57
  141.7 5.6 %collective-permute-start.3 = (bf16[128,512]{1,0:T(8,128)(2,1)S(1)}, bf16[128,512]{1,0:T(8,128)(2,1)S(1)}, u32[]{:S(2)}, u32[]{:S(2)}) collective-permute-start(bf16[128,512]{1,0:T(8,128)(2,1)S(1)} %collective-permute-done.1), channel_id=1, source_target_pairs={{0,7},{1,0},{2,1},{3,2},{4,3},{5,4},{6,5},{7,6},{8,15},{9,8},{10,9... | collective-permute-start | bytes 393224 | tf_op jit(solution)/shard_map/ppermute | solution.py:62
  147.3 5.6 %collective-permute-start.4 = (bf16[128,512]{1,0:T(8,128)(2,1)S(1)}, bf16[128,512]{1,0:T(8,128)(2,1)S(1)}, u32[]{:S(2)}, u32[]{:S(2)}) collective-permute-start(bf16[128,512]{1,0:T(8,128)(2,1)S(1)} %collective-permute-done.2), channel_id=1, source_target_pairs={{0,1},{1,2},{2,3},{3,4},{4,5},{5,6},{6,7},{7,0},{8,9},{9,10},{10,1... | collective-permute-start | bytes 393224 | tf_op jit(solution)/shard_map/ppermute | solution.py:57
  147.3 5.6 %collective-permute-start.5 = (bf16[128,512]{1,0:T(8,128)(2,1)S(1)}, bf16[128,512]{1,0:T(8,128)(2,1)S(1)}, u32[]{:S(2)}, u32[]{:S(2)}) collective-permute-start(bf16[128,512]{1,0:T(8,128)(2,1)S(1)} %collective-permute-done.3), channel_id=1, source_target_pairs={{0,7},{1,0},{2,1},{3,2},{4,3},{5,4},{6,5},{7,6},{8,15},{9,8},{10,9... | collective-permute-start | bytes 393224 | tf_op jit(solution)/shard_map/ppermute | solution.py:62
  152.9 5.6 %collective-permute-start.6 = (bf16[128,512]{1,0:T(8,128)(2,1)S(1)}, bf16[128,512]{1,0:T(8,128)(2,1)S(1)}, u32[]{:S(2)}, u32[]{:S(2)}) collective-permute-start(bf16[128,512]{1,0:T(8,128)(2,1)S(1)} %collective-permute-done.4), channel_id=1, source_target_pairs={{0,1},{1,2},{2,3},{3,4},{4,5},{5,6},{6,7},{7,0},{8,9},{9,10},{10,1... | collective-permute-start | bytes 393224 | tf_op jit(solution)/shard_map/ppermute | solution.py:57
Sparse Core Ops, SparseCore 0:
  9.9 54.8 all-gather.1
  72.5 36.3 reduce-scatter.1
